TPU v7x, 512 devices: a whole 4x4x16 slice. The times are simulated.
512 devices in a mesh: row: 16 (over y, z_hi, core), col: 32 (over z_lo, x).
Axes of the slice: x: 4, y: 4, z: 16 (z_hi: 2, z_lo: 8; z = z_hi * 8 + z_lo), core: 2. Of those that a mesh axis runs over, the one named last changes fastest.
Arguments:
- images: bfloat16 [4096, 1024], P(('row', 'col')), may hold values from -6 to 6
- texts: bfloat16 [4096, 1024], P(('row', 'col')), may hold values from -6 to 6
- loss_weights: float32 [2], replicated, may hold values from 0.5 to 1.5
Outputs:
- grad_images: float32 [4096, 1024], P(('row', 'col'))
- grad_texts: float32 [4096, 1024], P(('row', 'col'))
All inputs are finite; a program needn't handle non-finite values.
Results may differ from a plain program's by a relative error of at most 0.0013.
Values may be sent and summed in bfloat16 or wider, within the bound.
A program may use at most 64 MiB of HBM per device.

v0:
```python
import math
import jax
import jax.numpy as jnp
from jax import lax
from jax.sharding import PartitionSpec as P


def local(images, texts, loss_weights):
    width = images.shape[1]
    batch = images.shape[0] * lax.axis_size("row") * lax.axis_size("col")
    scale = 1.0 / math.sqrt(width * batch)
    cross_scale = loss_weights[0] * scale
    inner_scale = loss_weights[1] * scale
    own = jnp.stack([images, texts])
    columns = lax.all_gather(own, "row", axis=1, tiled=True)
    col_img = columns[0]
    col_txt = columns[1]
    col_count = col_img.shape[0]
    keys = jnp.concatenate(
        [
            jnp.concatenate([col_txt, -col_img], axis=1),
            jnp.concatenate([col_img, -col_txt], axis=1),
        ],
        axis=0,
    )
    piece = lax.all_gather(own, "col", axis=1, tiled=True)
    joined = jnp.concatenate([piece[0], piece[1]], axis=1)
    scores = lax.dot_general(
        joined, keys, (((1,), (1,)), ((), ())), preferred_element_type=jnp.float32
    )
    p_mat = (scores[:, :col_count] * cross_scale).astype(jnp.bfloat16)
    q_mat = (scores[:, col_count:] * inner_scale).astype(jnp.bfloat16)
    joined, weights = (joined, jnp.concatenate([p_mat, q_mat], axis=1))
    result = jnp.dot(weights, keys, preferred_element_type=jnp.float32)
    terms = jnp.stack([result[:, :width], result[:, width:]])
    grads = lax.psum_scatter(terms, "col", scatter_dimension=1, tiled=True)
    return (grads[0], grads[1])


def solution(mesh):
    in_specs = (P(("row", "col"), None), P(("row", "col"), None), P())
    out_specs = (P(("row", "col"), None), P(("row", "col"), None))
    return jax.shard_map(local, mesh=mesh, in_specs=in_specs, out_specs=out_specs, check_vma=False)
```

profile of v0, /device:TPU:8, one launch (start us, length us, event | category | flops | bytes accessed | tf_op | source)
XLA Modules:
  0.0 497.0 jit_solution(4307591087020093460)
XLA Ops:
  7.2 0.0 all-gather.2.cloned.1.call-start
  7.2 1.4 pad_maximum_fusion.1
  8.6 0.0 all-gather.2.cloned.1.call-update
  8.6 0.0 reduce-scatter.2.cloned.1.call-start
  8.6 1.3 fusion.14
  11.2 54.2 %all_gather.7 = bf16[2,128,1024]{2,1,0:T(8,128)(2,1)S(1)} all-gather(bf16[2,8,1024]{2,1,0:T(8,128)(2,1)} %pad_maximum_fusion.1), channel_id=1, replica_groups=mesh['row'=16,'col'=32] {'row'}, dimensions={1}, use_global_device_ids=true | all-gather | bytes 557056 | tf_op jit(solution)/shard_map/all_gather | solution.py:15
  65.5 173.2 %all-gather.2.cloned.1.call-done = bf16[2,256,1024]{2,1,0:T(8,128)(2,1)} async-done(((bf16[2,8,1024]{2,1,0:T(8,128)(2,1)}), bf16[2,256,1024]{2,1,0:T(8,128)(2,1)}) %all-gather.2.cloned.1.call-update) | async-done | bytes 1048592 | tf_op jit(solution)/shard_map/all_gather | solution.py:26
  238.6 1.3 slice_bitcast_fusion.3
  239.9 0.6 fusion
  240.5 0.5 fusion.4
  241.0 0.2 slice_bitcast_fusion.1
  241.2 1.5 pad_maximum_fusion
  242.7 0.0 reduce-scatter.2.cloned.1.call-update
  242.7 246.1 %reduce-scatter.2.cloned.1.call-done = f32[2,8,1024]{2,1,0:T(8,128)} async-done(((f32[2,256,1024]{2,1,0:T(8,128)}), f32[2,8,1024]{2,1,0:T(8,128)}) %reduce-scatter.2.cloned.1.call-update) | async-done | bytes 65552 | tf_op jit(solution)/shard_map/reduce_scatter | solution.py:36
  488.8 1.4 slice_bitcast_fusion.6
  (3 shorter events, 0.1 us)
Async XLA Ops:
  7.2 231.5 %all-gather.2.cloned.1.call-start = ((), (), s32[]{:S(2)}) async-start(), calls=%async_computation.1 | async-start | bytes 1081344 | tf_op jit(solution)/shard_map/all_gather | solution.py:26
  8.6 480.2 %reduce-scatter.2.cloned.1.call-start = ((), (), s32[]{:S(2)}) async-start(), calls=%async_computation.2 | async-start | bytes 2162688 | tf_op jit(solution)/shard_map/reduce_scatter | solution.py:36
Sparse Core Ops, SparseCore 0:
  10.6 227.9 all-gather.1
  242.8 245.9 reduce-scatter.1
where the time goes:
time: 497 us
  waiting for transfers between devices  419 us (84%)
  blocking collectives  54.2 us (11%)
  between operations  15.3 us (3%)
    reduce_scatter x1, waiting for transfers between devices, local(): grads = lax.psum_scatter(terms, 'col', scatter_dimension=1, tiled=True)  246 us
    all_gather x1, waiting for transfers between devices, local(): piece = lax.all_gather(own, 'col', axis=1, tiled=True)  173 us
    all_gather x1, blocking collectives, local(): columns = lax.all_gather(own, 'row', axis=1, tiled=True)  54.2 us
  transfers between devices with their start and end apart: 2, of which 2 were waited for; matrix products, arithmetic and copies ran while one was open for 0% of the time, Pallas kernels for 0%

commit v1 on v0

--- a/solution.py
+++ b/solution.py
@@ -23,7 +23,15 @@
         ],
         axis=0,
     )
-    piece = lax.all_gather(own, "col", axis=1, tiled=True)
+    piece = jnp.concatenate(
+        lax.all_to_all(
+            jnp.stack([own for _ in range(lax.axis_size("col"))]),
+            axis_name="col",
+            split_axis=0,
+            concat_axis=0,
+        ),
+        axis=1,
+    )
     joined = jnp.concatenate([piece[0], piece[1]], axis=1)
     scores = lax.dot_general(
         joined, keys, (((1,), (1,)), ((), ())), preferred_element_type=jnp.float32

time: 497 us -> 366 us (0.74)
  waiting for transfers between devices: 419 us -> 276 us
  starting transfers between devices: 0.08 us -> 15.4 us
    all_gather x1 -> x0, waiting for transfers between devices: 173 us -> none  [local(): piece = lax.all_gather(own, 'col', axis=1, tiled=True)]
    reduce_scatter x1, waiting for transfers between devices: 246 us -> 263 us  [local(): grads = lax.psum_scatter(terms, 'col', scatter_dimension=1, tiled=True)]
    all_to_all x0 -> x1, starting transfers between devices: none -> 15.4 us  [local(): lax.all_to_all(jnp.stack([own for _ in range(lax.axis_size('col'))]), axi...]
    all_to_all x0 -> x1, waiting for transfers between devices: none -> 13.6 us  [local(): lax.all_to_all(jnp.stack([own for _ in range(lax.axis_size('col'))]), axi...]
where the time goes in v1:
time: 366 us; the launch traced here: 365 us
  waiting for transfers between devices  276 us (75%)
  blocking collectives  51.7 us (14%)
  starting transfers between devices  15.4 us (4%)
  between operations  15.4 us (4%)
    reduce_scatter x1, waiting for transfers between devices, local(): grads = lax.psum_scatter(terms, 'col', scatter_dimension=1, tiled=True)  263 us
    all_gather x1, blocking collectives, local(): columns = lax.all_gather(own, 'row', axis=1, tiled=True)  51.7 us
    all_to_all x1, starting transfers between devices, local(): lax.all_to_all(jnp.stack([own for _ in range(lax.axis_size('col'))]), axi...  15.4 us
    all_to_all x1, waiting for transfers between devices, local(): lax.all_to_all(jnp.stack([own for _ in range(lax.axis_size('col'))]), axi...  13.6 us
  transfers between devices with their start and end apart: 2, of which 2 were waited for; matrix products, arithmetic and copies ran while one was open for 0% of the time, Pallas kernels for 0%

profile of v1, /device:TPU:8, one launch (start us, length us, event | category | flops | bytes accessed | tf_op | source)
XLA Modules:
  0.0 365.5 jit_solution(17684801559719878337)
XLA Ops:
  7.2 0.0 copy-start
  7.2 0.7 pad_maximum_fusion.1
  7.9 1.1 stack.17
  9.0 15.4 %all-to-all-start = ((bf16[32,2,8,1024]{3,2,1,0:T(8,128)(2,1)}), bf16[32,2,8,1024]{3,2,1,0:T(8,128)(2,1)S(1)}, u32[]{:S(2)}, u32[]{:S(2)}) async-start(bf16[32,2,8,1024]{3,2,1,0:T(8,128)(2,1)} %stack.17), calls=%async_computation | async-start | bytes 2097152 | tf_op jit(solution)/shard_map/all_to_all | solution.py:27
  24.4 0.0 reduce-scatter.2.cloned.1.call-start
  24.5 0.0 copy-done
  24.5 0.6 fusion.14
  26.3 51.7 %all_gather.3 = bf16[2,128,1024]{2,1,0:T(8,128)(2,1)S(1)} all-gather(bf16[2,8,1024]{2,1,0:T(8,128)(2,1)S(1)} %pad_maximum_fusion.1), channel_id=1, replica_groups=mesh['row'=16,'col'=32] {'row'}, dimensions={1}, use_global_device_ids=true | all-gather | bytes 557056 | tf_op jit(solution)/shard_map/all_gather | solution.py:15
  78.1 13.6 %all-to-all-done = bf16[32,2,8,1024]{3,2,1,0:T(8,128)(2,1)S(1)} async-done(((bf16[32,2,8,1024]{3,2,1,0:T(8,128)(2,1)}), bf16[32,2,8,1024]{3,2,1,0:T(8,128)(2,1)S(1)}, u32[]{:S(2)}, u32[]{:S(2)}) %all-to-all-start) | async-done | bytes 1048608 | tf_op jit(solution)/shard_map/all_to_all | solution.py:27
  91.8 0.1 slice_bitcast_fusion.3
  91.8 0.6 fusion
  92.4 0.5 fusion.4
  92.9 0.1 slice_bitcast_fusion.1
  93.0 1.6 pad_maximum_fusion
  94.6 0.0 reduce-scatter.2.cloned.1.call-update
  94.7 262.6 %reduce-scatter.2.cloned.1.call-done = f32[2,8,1024]{2,1,0:T(8,128)} async-done(((f32[2,256,1024]{2,1,0:T(8,128)}), f32[2,8,1024]{2,1,0:T(8,128)}) %reduce-scatter.2.cloned.1.call-update) | async-done | bytes 65552 | tf_op jit(solution)/shard_map/reduce_scatter | solution.py:44
  357.2 1.4 slice_bitcast_fusion.6
  (3 shorter events, 0.1 us)
Async XLA Ops:
  7.2 17.3 %copy-start = (f32[2]{0:T(128)S(1)}, f32[2]{0:T(128)}, u32[]{:S(2)}) copy-start(f32[2]{0:T(128)} %param.5) | copy-start | bytes 28
  9.0 82.7 %all-to-all-start = ((bf16[32,2,8,1024]{3,2,1,0:T(8,128)(2,1)}), bf16[32,2,8,1024]{3,2,1,0:T(8,128)(2,1)S(1)}, u32[]{:S(2)}, u32[]{:S(2)}) async-start(bf16[32,2,8,1024]{3,2,1,0:T(8,128)(2,1)} %stack.17), calls=%async_computation | async-start | bytes 2097152 | tf_op jit(solution)/shard_map/all_to_all | solution.py:27
  24.4 332.8 %reduce-scatter.2.cloned.1.call-start = ((), (), s32[]{:S(2)}) async-start(), calls=%async_computation.2 | async-start | bytes 2162688 | tf_op jit(solution)/shard_map/reduce_scatter | solution.py:44
Sparse Core Ops, SparseCore 0:
  94.8 262.4 reduce-scatter.1
